TPU v7x, 256 devices: a whole 4x4x8 slice. The times are simulated.
256 devices in a mesh: expert: 64 (over z, y, core), tensor: 4 (over x).
Axes of the slice: x: 4, y: 4, z: 8, core: 2. Of those that a mesh axis runs over, the one named last changes fastest.
Arguments:
- tokens: bfloat16 [4096, 4096], P('expert', 'tensor'), may hold values from -6 to 6
- grad_out: bfloat16 [4096, 4096], P('expert', 'tensor'), may hold values from -6 to 6
- expert_ids: int32 [4096, 8], P('expert'), may hold values from 0 to 63, all different within a row; in each aligned block of 64 rows (0 to 63, 64 to 127, ...) at most 9 rows name the same one
- route_weights: bfloat16 [4096, 8], P('expert'), may hold values from 0.049804688 to 1
- gate_weights: bfloat16 [64, 4096, 1536], P('expert', None, 'tensor'), may hold values from -0.09375 to 0.09375
- up_weights: bfloat16 [64, 4096, 1536], P('expert', None, 'tensor'), may hold values from -0.09375 to 0.09375
- down_weights: bfloat16 [64, 1536, 4096], P('expert', 'tensor'), may hold values from -0.15625 to 0.15625
Outputs:
- grad_tokens: bfloat16 [4096, 4096], P('expert', 'tensor')
- grad_weights: bfloat16 [4096, 8], P('expert')
Inputs may be any that keep to these rules, and one draw needn't show every extreme that they name: `expert_ids`: each row names 8 different experts. Among the 64 rows of one index of expert no expert is named by more than 9 rows, and in every draw some expert is named by exactly 9 rows of one index.
All inputs are finite; a program needn't handle non-finite values.
Results may differ from a plain program's by a relative error of at most 0.008.
Values may be sent and summed in bfloat16 or wider, within the bound.
A program may use at most 128 MiB of HBM per device.

v0:
```python
import jax
import jax.numpy as jnp
from jax import lax
from jax.sharding import PartitionSpec as P

TOP = 8


def route_slots(flat_ids, experts, capacity):
    onehot = (flat_ids[:, None] == jnp.arange(experts, dtype=jnp.int32)[None, :]).astype(jnp.int32)
    before = jnp.cumsum(onehot, axis=0) - onehot
    position = jnp.sum(before * onehot, axis=1)
    target = flat_ids * capacity + position
    routes = flat_ids.shape[0]
    return (
        jnp.full((experts * capacity,), -1, jnp.int32)
        .at[target]
        .set(jnp.arange(routes, dtype=jnp.int32))
    )


def expert_block(inputs, grads, scales, gate_weight, up_weight, down_weight):
    contract = (((1,), (1,)), ((), ()))
    gate_vals = jnp.dot(inputs, gate_weight, preferred_element_type=jnp.float32)
    up_vals = jnp.dot(inputs, up_weight, preferred_element_type=jnp.float32)
    back_vals = lax.dot_general(grads, down_weight, contract, preferred_element_type=jnp.float32)
    sigmoid = jax.nn.sigmoid(gate_vals)
    active = gate_vals * sigmoid
    weight_grad = jnp.sum(active * up_vals * back_vals, axis=1)
    scaled = scales[:, None] * back_vals
    gate_grad = (scaled * up_vals * sigmoid * (1.0 + gate_vals * (1.0 - sigmoid))).astype(
        jnp.bfloat16
    )
    up_grad = (scaled * active).astype(jnp.bfloat16)
    input_grad = lax.dot_general(
        gate_grad, gate_weight, contract, preferred_element_type=jnp.float32
    )
    input_grad = input_grad + lax.dot_general(
        up_grad, up_weight, contract, preferred_element_type=jnp.float32
    )
    return (input_grad.astype(jnp.bfloat16), weight_grad)


def block_size(total):
    size = 256
    while total % size:
        size = size // 2
    return size


def fill_slots(source_rows, live_mask, owner_rows):
    return jnp.where(live_mask[:, None], source_rows[owner_rows], jnp.zeros((), source_rows.dtype))


def dense_rows(inputs, grads, scales, gate_weight, up_weight, down_weight):
    total = inputs.shape[0]
    size = block_size(total)
    count = total // size

    def one_block(pieces):
        return expert_block(pieces[0], pieces[1], pieces[2], gate_weight, up_weight, down_weight)

    grad_rows, weight_rows = lax.map(
        one_block,
        (
            inputs.reshape(count, size, -1),
            grads.reshape(count, size, -1),
            scales.reshape(count, size),
        ),
    )
    return (grad_rows.reshape(total, -1), weight_rows.reshape(total))


def body(tokens, grad_out, expert_ids, route_weights, gate_weights, up_weights, down_weights):
    experts = lax.axis_size("expert")
    tok_rows = tokens.shape[0]
    capacity = min(tok_rows, max(2, 7 * tok_rows * TOP // (6 * experts)))
    slot_route = route_slots(expert_ids.reshape(-1), experts, capacity)
    live_mask = slot_route >= 0
    safe_route = jnp.where(live_mask, slot_route, 0)
    owner_rows = safe_route // TOP
    slot_scale = jnp.where(
        live_mask, route_weights.reshape(-1)[safe_route], jnp.zeros((), jnp.bfloat16)
    )
    full_tokens, full_grads = (
        lax.all_gather(tokens, "tensor", axis=1, tiled=True),
        lax.all_gather(grad_out, "tensor", axis=1, tiled=True),
    )
    sent = (
        fill_slots(full_tokens, live_mask, owner_rows),
        fill_slots(full_grads, live_mask, owner_rows),
        slot_scale,
    )
    got_tokens, got_grads, got_scale = (
        lax.all_to_all(sent[0], "expert", split_axis=0, concat_axis=0, tiled=True),
        lax.all_to_all(sent[1], "expert", split_axis=0, concat_axis=0, tiled=True),
        lax.all_to_all(sent[2], "expert", split_axis=0, concat_axis=0, tiled=True),
    )
    scales = got_scale.astype(jnp.float32)
    gate_weight = gate_weights[0]
    up_weight = up_weights[0]
    down_weight = down_weights[0]
    grad_rows, weight_rows = dense_rows(
        got_tokens, got_grads, scales, gate_weight, up_weight, down_weight
    )
    weight_total = lax.psum(weight_rows, "tensor").astype(jnp.bfloat16)
    select = (owner_rows[None, :] == jnp.arange(tok_rows, dtype=jnp.int32)[:, None]) & live_mask[
        None, :
    ]
    back_grads, back_weights = (
        lax.all_to_all(grad_rows, "expert", split_axis=0, concat_axis=0, tiled=True),
        lax.all_to_all(weight_total, "expert", split_axis=0, concat_axis=0, tiled=True),
    )
    partial_sum = jnp.dot(
        select.astype(jnp.bfloat16), back_grads, preferred_element_type=jnp.float32
    )
    input_grads = lax.psum_scatter(partial_sum, "tensor", scatter_dimension=1, tiled=True).astype(
        jnp.bfloat16
    )
    target = jnp.where(live_mask, slot_route, tok_rows * TOP)
    route_grads = (
        jnp.zeros((tok_rows * TOP,), jnp.bfloat16).at[target].set(back_weights, mode="drop")
    )
    return (input_grads, route_grads.reshape(tok_rows, TOP))


def solution(mesh):
    in_specs = (
        P("expert", "tensor"),
        P("expert", "tensor"),
        P("expert", None),
        P("expert", None),
        P("expert", None, "tensor"),
        P("expert", None, "tensor"),
        P("expert", "tensor", None),
    )
    out_specs = (P("expert", "tensor"), P("expert", None))
    return jax.shard_map(body, mesh=mesh, in_specs=in_specs, out_specs=out_specs, check_vma=False)
```

profile of v0, /device:TPU:1, one launch (start us, length us, event | category | flops | bytes accessed | tf_op | source)
XLA Modules:
  0.0 840.5 jit_solution(10379291527371922853)
XLA Ops:
  10.6 2.4 scatter_custom_fusion
  14.0 3.9 gather_fusion
  18.7 13.2 %all-to-all-start = ((bf16[64,9,1]{1,2,0:T(2,128)(2,1)}), bf16[64,9,1]{1,2,0:T(2,128)(2,1)S(1)}, u32[]{:S(2)}, u32[]{:S(2)}) async-start(bf16[64,9,1]{1,2,0:T(2,128)(2,1)} %all_to_all.40), calls=%async_computation | async-start | bytes 65536 | tf_op jit(solution)/shard_map/all_to_all | solution.py:97
  31.9 11.3 %all_gather.6 = bf16[64,4096]{1,0:T(8,128)(2,1)S(1)} all-gather(bf16[64,1024]{1,0:T(8,128)(2,1)} %param.10), channel_id=1, replica_groups=mesh['expert'=64,'tensor'=4] {'tensor'}, dimensions={1}, use_global_device_ids=true | all-gather | bytes 655360 | tf_op jit(solution)/shard_map/all_gather | solution.py:87
  43.2 5.3 gather_fusion.1
  48.5 8.1 gather.15
  56.6 9.9 %all_gather.7 = bf16[64,4096]{1,0:T(8,128)(2,1)S(1)} all-gather(bf16[64,1024]{1,0:T(8,128)(2,1)S(1)} %copy-done.3), channel_id=1, replica_groups=mesh['expert'=64,'tensor'=4] {'tensor'}, dimensions={1}, use_global_device_ids=true | all-gather | bytes 655360 | tf_op jit(solution)/shard_map/all_gather | solution.py:86
  66.5 5.2 gather_fusion.2
  71.7 8.2 gather.17
  80.0 11.4 %broadcast_select_fusion = (bf16[64,9,4096]{2,1,0:T(8,128)(2,1)}, bf16[64,9,4096]{2,1,0:T(8,128)(2,1)}) fusion(bf16[64,9,4096]{2,1,0:T(8,128)(2,1)} %gather.17, pred[64,9]{1,0:T(8,128)(4,1)S(1)} %broadcast_in_dim.68, bf16[64,9,4096]{2,1,0:T(8,128)(2,1)} %gather.15), kind=kLoop, calls=%fused_computation.34 | loop fusion | flops 4718592 | bytes 18874944 | tf_op jit(solution)/shard_map/jit(_where)/select_n | solution.py:52
  91.4 200.1 %all_to_all.47 = bf16[64,9,4096]{2,1,0:T(8,128)(2,1)} all-to-all(bf16[64,9,4096]{2,1,0:T(8,128)(2,1)} %get-tuple-element.79), channel_id=1, replica_groups=mesh['expert'=64,'tensor'=4] {'expert'}, dimensions={0} | all-to-all | bytes 9437184 | tf_op jit(solution)/shard_map/all_to_all | solution.py:96
  291.5 7.3 all-to-all-start.2
  299.3 8.4 %reshape.101 = bf16[9,64,4096]{2,1,0:T(8,128)(2,1)} reshape(bf16[64,9,4096]{2,1,0:T(8,128)(2,1)} %all_to_all.47) | data formatting | bytes 9437184 | tf_op jit(solution)/shard_map/reshape | solution.py:67
  307.7 174.0 %all-to-all-done.2 = bf16[64,9,4096]{2,1,0:T(8,128)(2,1)} async-done(((bf16[64,9,4096]{2,1,0:T(8,128)(2,1)}), bf16[64,9,4096]{2,1,0:T(8,128)(2,1)}, u32[]{:S(2)}, u32[]{:S(2)}) %all-to-all-start.2) | async-done | bytes 4718624 | tf_op jit(solution)/shard_map/all_to_all | solution.py:95
  481.7 8.5 %reshape.102 = bf16[9,64,4096]{2,1,0:T(8,128)(2,1)} reshape(bf16[64,9,4096]{2,1,0:T(8,128)(2,1)} %all-to-all-done.2) | data formatting | bytes 9437184 | tf_op jit(solution)/shard_map/reshape | solution.py:66
  490.2 89.7 %while.12 = (s32[]{:T(128)}, bf16[9,64,4096]{2,1,0:T(8,128)(2,1)}, f32[9,64]{1,0:T(8,128)S(1)}, f32[9,64]{1,0:T(8,128)S(1)}, bf16[9,64,4096]{2,1,0:T(8,128)(2,1)...) while((s32[]{:T(128)}, bf16[9,64,4096]{2,1,0:T(8,128)(2,1)}, ...), condition=%wide.region_6.7_spmd, body=%wide.region_4.6_spmd.sunk | while | flops 1007771584 | bytes 46075820 | solution.py:63
  492.0 2.6 fusion.65
  494.7 2.4 multiply_reduce_fusion.2
  498.2 2.0 fusion.68
  502.0 2.6 fusion.65
  504.7 2.4 multiply_reduce_fusion.2
  512.0 2.6 fusion.65
  514.6 2.4 multiply_reduce_fusion.2
  518.2 1.9 fusion.68
  521.9 2.6 fusion.65
  524.6 2.4 multiply_reduce_fusion.2
  528.1 1.9 fusion.68
  531.9 2.6 fusion.65
  534.6 2.4 multiply_reduce_fusion.2
  538.1 1.9 fusion.68
  541.8 2.6 fusion.65
  544.5 2.4 multiply_reduce_fusion.2
  551.8 2.6 fusion.65
  554.5 2.4 multiply_reduce_fusion.2
  558.0 1.9 fusion.68
  561.8 2.6 fusion.65
  564.4 2.4 multiply_reduce_fusion.2
  568.0 1.9 fusion.68
  571.7 2.6 fusion.65
  574.4 2.4 multiply_reduce_fusion.2
  577.9 1.9 fusion.68
  579.9 8.1 all_to_all.34
  588.0 194.3 %all_to_all.48 = bf16[64,9,4096]{2,1,0:T(8,128)(2,1)} all-to-all(bf16[64,9,4096]{2,1,0:T(8,128)(2,1)} %all_to_all.34), channel_id=1, replica_groups=mesh['expert'=64,'tensor'=4] {'expert'}, dimensions={0} | all-to-all | bytes 9437184 | tf_op jit(solution)/shard_map/all_to_all | solution.py:111
  782.3 8.5 %all_to_all.36 = bf16[576,4096]{1,0:T(8,128)(2,1)} reshape(bf16[64,9,4096]{2,1,0:T(8,128)(2,1)} %all_to_all.48) | data formatting | bytes 9437184 | tf_op jit(solution)/shard_map/all_to_all | solution.py:111
  790.8 4.4 fusion.25
  795.3 8.8 %psum.7 = bf16[576]{0:T(1024)(128)(2,1)S(1)} all-reduce(f32[576]{0:T(1024)S(1)} %reshape.103), channel_id=1, replica_groups=mesh['expert'=64,'tensor'=4] {'tensor'}, use_global_device_ids=true, to_apply=%region_8.9 | all-reduce | flops 576 | bytes 3456 | tf_op jit(solution)/shard_map/psum | solution.py:106
  804.2 18.2 %all_to_all.49 = bf16[64,9,1]{1,2,0:T(2,128)(2,1)S(1)} all-to-all(bf16[64,9,1]{1,2,0:T(2,128)(2,1)S(1)} %all_to_all.41), channel_id=1, replica_groups=mesh['expert'=64,'tensor'=4] {'expert'}, dimensions={0} | all-to-all | bytes 2304 | tf_op jit(solution)/shard_map/all_to_all | solution.py:112
  822.7 8.6 %scatter_custom_fusion.1 = bf16[512]{0:T(512)(128)(2,1)S(1)} fusion(s32[576]{0:T(1024)S(1)} %get-tuple-element.80, bf16[576]{0:T(1024)(128)(2,1)S(1)} %reshape.142, bf16[]{:T(256)} %constant.53.clone.1), kind=kCustom, calls=%fused_computation.69 | custom fusion | bytes 1026 | tf_op jit(solution)/shard_map/scatter | solution.py:122
  (116 shorter events, 38.9 us)
Async XLA Ops:
  18.7 72.7 %all-to-all-start = ((bf16[64,9,1]{1,2,0:T(2,128)(2,1)}), bf16[64,9,1]{1,2,0:T(2,128)(2,1)S(1)}, u32[]{:S(2)}, u32[]{:S(2)}) async-start(bf16[64,9,1]{1,2,0:T(2,128)(2,1)} %all_to_all.40), calls=%async_computation | async-start | bytes 65536 | tf_op jit(solution)/shard_map/all_to_all | solution.py:97
  48.5 8.1 copy-start.3
  291.5 190.2 %all-to-all-start.2 = ((bf16[64,9,4096]{2,1,0:T(8,128)(2,1)}), bf16[64,9,4096]{2,1,0:T(8,128)(2,1)}, u32[]{:S(2)}, u32[]{:S(2)}) async-start(bf16[64,9,4096]{2,1,0:T(8,128)(2,1)} %get-tuple-element.78), calls=%async_computation.2 | async-start | bytes 16777216 | tf_op jit(solution)/shard_map/all_to_all | solution.py:95
  298.8 533.2 %reduce-scatter.2.cloned.1.call-start = ((), (), s32[]{:S(2)}) async-start(), calls=%async_computation.6 | async-start | bytes 1310720 | tf_op jit(solution)/shard_map/reduce_scatter | solution.py:117
  307.7 182.5 %copy-start = (bf16[1,4096,384]{2,1,0:T(8,128)(2,1)S(1)}, bf16[1,4096,384]{2,1,0:T(8,128)(2,1)}, u32[]{:S(2)}) copy-start(bf16[1,4096,384]{2,1,0:T(8,128)(2,1)} %param.13) | copy-start | bytes 9437188
  490.2 4.4 copy-start.2
  494.6 3.6 copy-start.1
  500.2 4.5 copy-start.2
  504.7 3.6 copy-start.1
  510.2 4.4 copy-start.2
  514.6 3.6 copy-start.1
  520.1 4.4 copy-start.2
  524.5 3.6 copy-start.1
  530.1 4.5 copy-start.2
  534.5 3.6 copy-start.1
  540.1 4.4 copy-start.2
  544.5 3.6 copy-start.1
  550.0 4.4 copy-start.2
  554.4 3.6 copy-start.1
  560.0 4.5 copy-start.2
  564.4 3.6 copy-start.1
  569.9 4.4 copy-start.2
  574.4 3.6 copy-start.1
Sparse Core Ops, SparseCore 0:
  795.3 22.6 reduce-scatter.1
where the time goes:
time: 842 us; the launch traced here: 841 us
  blocking collectives  443 us (53%)
  waiting for transfers between devices  174 us (21%)
  matrix products  93 us (11%)
  local copies, waits for them, and re-layouts  80.2 us (10%)
  starting transfers between devices  20.6 us (2%)
  other arithmetic  15.4 us (2%)
  between operations  14.2 us (2%)
    all_to_all x1, blocking collectives, body(): lax.all_to_all(sent[1], 'expert', split_axis=0, concat_axis=0, tiled=True)  200 us
    all_to_all x1, blocking collectives, body(): lax.all_to_all(grad_rows, 'expert', split_axis=0, concat_axis=0, tiled=True)  194 us
    all_to_all x1, waiting for transfers between devices, body(): lax.all_to_all(sent[0], 'expert', split_axis=0, concat_axis=0, tiled=True)  174 us
    gather x4, local copies, waits for them, and re-layouts, fill_slots(): source_rows[owner_rows]  26.7 us
    dot_general x9, matrix products, expert_block(): up_vals = jnp.dot(inputs, up_weight, preferred_element_type=jnp.float32)  23.7 us
    dot_general x9, matrix products, expert_block(): lax.dot_general(grads, down_weight, contract, preferred_element_type=jnp....  21.5 us
    all_to_all x1, blocking collectives, body(): lax.all_to_all(weight_total, 'expert', split_axis=0, concat_axis=0, tiled...  18.2 us
    dot_general x9, matrix products, expert_block(): lax.dot_general(up_grad, up_weight, contract, preferred_element_type=jnp....  17.4 us
  transfers between devices with their start and end apart: 3, of which 1 were waited for; matrix products, arithmetic and copies ran while one was open for 7% of the time, Pallas kernels for 0%

commit v1 on v0

v1 whole, which is shorter than its diff:
```python
import jax
import jax.numpy as jnp
from jax import lax
from jax.sharding import PartitionSpec as P

TOP = 8


def expert_rows(inputs, grads, scales, gate_weight, up_weight, down_weight):
    contract = (((1,), (1,)), ((), ()))
    gate_vals = jnp.dot(inputs, gate_weight, preferred_element_type=jnp.float32)
    up_vals = jnp.dot(inputs, up_weight, preferred_element_type=jnp.float32)
    back_vals = lax.dot_general(grads, down_weight, contract, preferred_element_type=jnp.float32)
    sigmoid = jax.nn.sigmoid(gate_vals)
    active = gate_vals * sigmoid
    weight_grad = jnp.sum(active * up_vals * back_vals, axis=1)
    scaled = scales * back_vals
    gate_grad = (scaled * up_vals * sigmoid * (1.0 + gate_vals * (1.0 - sigmoid))).astype(
        jnp.bfloat16
    )
    up_grad = (scaled * active).astype(jnp.bfloat16)
    input_grad = lax.dot_general(
        gate_grad, gate_weight, contract, preferred_element_type=jnp.float32
    )
    input_grad = input_grad + lax.dot_general(
        up_grad, up_weight, contract, preferred_element_type=jnp.float32
    )
    return input_grad.astype(jnp.bfloat16), weight_grad


def body(tokens, grad_out, expert_ids, route_weights, gate_weights, up_weights, down_weights):
    experts = lax.axis_size("expert")
    rows, width = tokens.shape
    capacity = min(rows, max(2, 7 * rows * TOP // (6 * experts)))
    hit = expert_ids[:, :, None] == jnp.arange(experts, dtype=jnp.int32)
    named = jnp.any(hit, axis=1)
    below = jnp.tril(jnp.ones((rows, rows), jnp.bfloat16), -1)
    place = jnp.dot(below, named.astype(jnp.bfloat16), preferred_element_type=jnp.float32)
    scale = jnp.sum(jnp.where(hit, route_weights[:, :, None].astype(jnp.float32), 0.0), axis=1)
    slot = jnp.arange(capacity, dtype=jnp.float32)
    select = named[:, :, None] & (place[:, :, None] == slot)
    picked = select.astype(jnp.bfloat16)
    spread = picked.reshape(rows, experts * capacity)
    slot_scale = jnp.sum(jnp.where(select, scale[:, :, None], 0.0), axis=0)
    both = jnp.concatenate([tokens, grad_out], axis=1)
    sent = lax.dot_general(
        spread, both, (((0,), (0,)), ((), ())), preferred_element_type=jnp.float32
    ).astype(jnp.bfloat16)
    tail = jnp.broadcast_to(slot_scale.reshape(-1, 1), (experts * capacity, 128))
    sent = jnp.concatenate([sent, tail.astype(jnp.bfloat16)], axis=1)
    got = lax.all_to_all(sent, "expert", split_axis=0, concat_axis=0, tiled=True)
    got_tokens = lax.all_gather(got[:, :width], "tensor", axis=1, tiled=True)
    got_grads = lax.all_gather(got[:, width : 2 * width], "tensor", axis=1, tiled=True)
    scales = got[:, 2 * width : 2 * width + 1].astype(jnp.float32)
    grad_rows, weight_rows = expert_rows(
        got_tokens, got_grads, scales, gate_weights[0], up_weights[0], down_weights[0]
    )
    weight_total = lax.psum(weight_rows, "tensor").astype(jnp.bfloat16)
    summed = lax.psum_scatter(grad_rows, "tensor", scatter_dimension=1, tiled=True)
    tail = jnp.broadcast_to(weight_total[:, None], (experts * capacity, 128))
    back = lax.all_to_all(
        jnp.concatenate([summed, tail], axis=1), "expert", split_axis=0, concat_axis=0, tiled=True
    )
    input_grads = jnp.dot(
        spread, back[:, :width], preferred_element_type=jnp.float32
    ).astype(jnp.bfloat16)
    route = back[:, width].astype(jnp.float32).reshape(experts, capacity)
    per_pair = jnp.sum(jnp.where(select, route, 0.0), axis=2)
    route_grads = jnp.sum(jnp.where(hit, per_pair[:, None, :], 0.0), axis=2)
    return input_grads, route_grads.astype(jnp.bfloat16)


def solution(mesh):
    in_specs = (
        P("expert", "tensor"),
        P("expert", "tensor"),
        P("expert", None),
        P("expert", None),
        P("expert", None, "tensor"),
        P("expert", None, "tensor"),
        P("expert", "tensor", None),
    )
    out_specs = (P("expert", "tensor"), P("expert", None))
    return jax.shard_map(body, mesh=mesh, in_specs=in_specs, out_specs=out_specs, check_vma=False)
```

time: 842 us -> 417 us (0.50)
  blocking collectives: 443 us -> 192 us
  matrix products: 93 us -> 27.7 us
  local copies, waits for them, and re-layouts: 80.2 us -> 29.4 us
  waiting for transfers between devices: 174 us -> 145 us
  starting transfers between devices: 20.6 us -> 0.3 us
    all_to_all x3 -> x2, blocking collectives: 413 us -> 185 us  [the longest x1 116 us: body(): lax.all_to_all(sent, 'expert', split_axis=0, concat_axis=0, tiled=True)]
    all_to_all x2 -> x0, waiting for transfers between devices: 174 us -> none  [the longest x1 174 us: body(): lax.all_to_all(sent[0], 'expert', split_axis=0, concat_axis=0, tiled=True)]
    all_gather x0 -> x2, waiting for transfers between devices: none -> 96.6 us  [the longest x1 48.7 us: body(): got_tokens = lax.all_gather(got[:, :width], 'tensor', axis=1, tiled=True)]
    dot_general x46 -> x8, matrix products: 93 us -> 27.7 us  [the longest x1 6.59 us: expert_rows(): lax.dot_general(grads, down_weight, contract, preferred_element_type=jnp....]
    reduce_scatter x1, waiting for transfers between devices: 0.01 us -> 47.6 us  [body(): lax.psum_scatter(grad_rows, 'tensor', scatter_dimension=1, tiled=True)]
    gather x5 -> x0, local copies, waits for them, and re-layouts: 30.7 us -> none  [the longest x4 26.7 us: fill_slots(): source_rows[owner_rows]]
    all_gather x2 -> x0, blocking collectives: 21.2 us -> none  [the longest x1 11.3 us: body(): lax.all_gather(grad_out, 'tensor', axis=1, tiled=True)]
    all_to_all x2 -> x0, starting transfers between devices: 20.4 us -> none  [the longest x1 13.2 us: body(): lax.all_to_all(sent[2], 'expert', split_axis=0, concat_axis=0, tiled=True)]
  transfers between devices with their start and end apart: 3 -> 3, of which waited for: 1 -> 3; matrix products, arithmetic and copies ran while one was open for 7% -> 3% of each run, Pallas kernels for 0% -> 0%
where the time goes in v1:
time: 417 us; the launch traced here: 416 us
  blocking collectives  192 us (46%)
  waiting for transfers between devices  145 us (35%)
  local copies, waits for them, and re-layouts  29.4 us (7%)
  matrix products  27.7 us (7%)
  between operations  13.9 us (3%)
  other arithmetic  8.48 us (2%)
    all_to_all x1, blocking collectives, body(): lax.all_to_all(sent, 'expert', split_axis=0, concat_axis=0, tiled=True)  116 us
    all_to_all x1, blocking collectives, body(): lax.all_to_all(jnp.concatenate([summed, tail], axis=1), 'expert', split_a...  68.8 us
    all_gather x1, waiting for transfers between devices, body(): got_tokens = lax.all_gather(got[:, :width], 'tensor', axis=1, tiled=True)  48.7 us
    all_gather x1, waiting for transfers between devices, body(): lax.all_gather(got[:, width:2 * width], 'tensor', axis=1, tiled=True)  47.9 us
    reduce_scatter x1, waiting for transfers between devices, body(): lax.psum_scatter(grad_rows, 'tensor', scatter_dimension=1, tiled=True)  47.6 us
    all_to_all x2, local copies, waits for them, and re-layouts, body(): lax.all_to_all(sent, 'expert', split_axis=0, concat_axis=0, tiled=True)  9.46 us
  transfers between devices with their start and end apart: 3, of which 3 were waited for; matrix products, arithmetic and copies ran while one was open for 3% of the time, Pallas kernels for 0%

profile of v1, /device:TPU:1, one launch (start us, length us, event | category | flops | bytes accessed | tf_op | source)
XLA Modules:
  0.0 416.4 jit_solution(18322527251276431889)
XLA Ops:
  7.2 0.0 all-gather.5.cloned.1.call-start
  7.2 0.9 copy.18
  8.2 0.2 fusion.22
  8.3 0.1 copy.19
  8.4 0.2 fusion.25
  8.7 0.8 copy.21
  9.4 0.2 select_reduce_fusion.3
  9.7 0.1 copy.22
  9.7 0.2 select_reduce_fusion.1
  10.0 0.7 convert_element_type.45
  10.7 0.8 eq.40
  11.5 1.1 eq.41
  12.6 0.7 and.13
  13.3 1.6 and.14
  15.0 0.7 eq.43
  15.7 1.0 compare_and_fusion
  16.7 1.7 convolution_convert_fusion
  18.5 0.8 broadcast_in_dim.72
  19.3 1.7 pad_maximum_fusion
  21.0 4.7 %all_to_all.16 = bf16[64,9,2176]{2,1,0:T(8,128)(2,1)} reshape(bf16[576,2176]{1,0:T(8,128)(2,1)} %pad_maximum_fusion) | data formatting | bytes 5013504 | tf_op jit(solution)/shard_map/all_to_all | solution.py:51
  25.7 116.2 %all_to_all.24 = bf16[64,9,2176]{2,1,0:T(8,128)(2,1)} all-to-all(bf16[64,9,2176]{2,1,0:T(8,128)(2,1)} %all_to_all.16), channel_id=1, replica_groups=mesh['expert'=64,'tensor'=4] {'expert'}, dimensions={0} | all-to-all | bytes 5013504 | tf_op jit(solution)/shard_map/all_to_all | solution.py:51
  142.0 4.8 %all_to_all.18 = bf16[576,2176]{1,0:T(8,128)(2,1)} reshape(bf16[64,9,2176]{2,1,0:T(8,128)(2,1)} %all_to_all.24) | data formatting | bytes 5013504 | tf_op jit(solution)/shard_map/all_to_all | solution.py:51
  146.7 3.3 fusion.35
  150.1 0.0 all-gather.3.cloned.1.call-start
  150.1 0.7 all-gather.3.cloned.1.call-update
  150.8 0.2 reduce-scatter.2.cloned.1.call-start
  151.0 1.1 convert_reduce_fusion.1
  152.1 48.7 %all-gather.5.cloned.1.call-done = bf16[576,4096]{1,0:T(8,128)(2,1)} async-done(((bf16[576,1024]{1,0:T(8,128)(2,1)}), bf16[576,4096]{1,0:T(8,128)(2,1)}) %all-gather.5.cloned.1.call-update) | async-done | bytes 4718608 | tf_op jit(solution)/shard_map/all_gather | solution.py:52
  200.8 6.0 %fusion.2 = f32[576,384]{1,0:T(8,128)} fusion(bf16[576,4096]{1,0:T(8,128)(2,1)} %all-gather.5.cloned.1.call-done, bf16[1,4096,384]{2,1,0:T(8,128)(2,1)S(1)} %copy-done), kind=kOutput, calls=%fused_computation.3 | convolution fusion | flops 1811939328 | bytes 8749056 | tf_op jit(solution)/shard_map/dot_general | solution.py:11
  206.8 3.5 fusion.5
  210.3 47.9 %all-gather.3.cloned.1.call-done = bf16[576,4096]{1,0:T(8,128)(2,1)} async-done(((bf16[576,1024]{1,0:T(8,128)(2,1)}), bf16[576,4096]{1,0:T(8,128)(2,1)}) %all-gather.3.cloned.1.call-update) | async-done | bytes 4718608 | tf_op jit(solution)/shard_map/all_gather | solution.py:53
  258.2 6.6 %multiply_reduce_fusion = (f32[576]{0:T(1024)S(1)}, f32[576,384]{1,0:T(8,128)S(1)}) fusion(f32[576,384]{1,0:T(8,128)} %fusion.5, f32[576,384]{1,0:T(8,128)} %fusion.2, bf16[576,4096]{1,0:T(8,128)(2,1)} %all-gather.3.cloned.1.call-done, bf16[1,384,4096]{2,1,0:T(8,128)(2,1)} %param.13), kind=kOutput, calls=%fused_computation.16 | convolution fusion | flops 1813487104 | bytes 10520832 | tf_op jit(solution)/shard_map/dot_general | solution.py:13
  264.8 2.8 fusion
  267.7 4.5 %add_convert_fusion = bf16[576,4096]{1,0:T(8,128)(2,1)} fusion(f32[576,4096]{1,0:T(8,128)S(1)} %fusion, bf16[1,4096,384]{2,1,0:T(8,128)(2,1)S(1)} %copy-done.3, f32[576,384]{1,0:T(8,128)S(1)} %get-tuple-element.7, f32[576]{0:T(1024)S(1)} %convert_reduce_fusion.1, f32[576,384]{1,0:T(8,128)S(1)} %copy-done.1), kind=kOutput, calls=%fused_computation | convolution fusion | flops 1818206208 | bytes 19073280 | tf_op jit(solution)/shard_map/dot_general | solution.py:25
  272.2 6.7 %psum.7 = bf16[576]{0:T(1024)(128)(2,1)S(1)} all-reduce(f32[576]{0:T(1024)S(1)} %get-tuple-element.6), channel_id=1, replica_groups=mesh['expert'=64,'tensor'=4] {'tensor'}, use_global_device_ids=true, to_apply=%region_5.6 | all-reduce | flops 576 | bytes 3456 | tf_op jit(solution)/shard_map/psum | solution.py:58
  279.0 47.6 %reduce-scatter.2.cloned.1.call-done = bf16[576,1024]{1,0:T(8,128)(2,1)} async-done(((bf16[576,4096]{1,0:T(8,128)(2,1)}), bf16[576,1024]{1,0:T(8,128)(2,1)}) %reduce-scatter.2.cloned.1.call-update) | async-done | bytes 1179664 | tf_op jit(solution)/shard_map/reduce_scatter | solution.py:59
  326.6 0.1 broadcast_in_dim.73
  326.7 2.4 pad_maximum_fusion.1
  329.2 3.4 all_to_all.19
  332.6 68.8 %all_to_all.25 = bf16[64,9,1152]{2,1,0:T(8,128)(2,1)} all-to-all(bf16[64,9,1152]{2,1,0:T(8,128)(2,1)} %all_to_all.19), channel_id=1, replica_groups=mesh['expert'=64,'tensor'=4] {'expert'}, dimensions={0} | all-to-all | bytes 2654208 | tf_op jit(solution)/shard_map/all_to_all | solution.py:61
  401.4 3.7 all_to_all.21
  405.1 1.1 convert_reduce_fusion
  406.2 2.3 fusion.11
  408.5 0.1 reshape.28
  408.6 0.3 select_reduce_fusion
  408.9 0.1 copy.23
  409.0 0.2 select_reduce_fusion.2
  409.3 0.7 copy.24
  (20 shorter events, 0.1 us)
Async XLA Ops:
  7.2 193.6 %copy-start = (bf16[1,4096,384]{2,1,0:T(8,128)(2,1)S(1)}, bf16[1,4096,384]{2,1,0:T(8,128)(2,1)}, u32[]{:S(2)}) copy-start(bf16[1,4096,384]{2,1,0:T(8,128)(2,1)} %param.11) | copy-start | bytes 9437188
  7.2 193.6 %all-gather.5.cloned.1.call-start = ((), (), s32[]{:S(2)}) async-start(), calls=%async_computation.4 | async-start | bytes 5898240 | tf_op jit(solution)/shard_map/all_gather | solution.py:52
  8.7 2.1 copy-start.5
  150.1 108.1 %all-gather.3.cloned.1.call-start = ((), (), s32[]{:S(2)}) async-start(), calls=%async_computation.3 | async-start | bytes 5898240 | tf_op jit(solution)/shard_map/all_gather | solution.py:53
  150.8 175.8 %reduce-scatter.2.cloned.1.call-start = ((), (), s32[]{:S(2)}) async-start(), calls=%async_computation.5 | async-start | bytes 5898240 | tf_op jit(solution)/shard_map/reduce_scatter | solution.py:59
  200.8 6.0 %copy-start.2 = (bf16[1,4096,384]{2,1,0:T(8,128)(2,1)S(1)}, bf16[1,4096,384]{2,1,0:T(8,128)(2,1)}, u32[]{:S(2)}) copy-start(bf16[1,4096,384]{2,1,0:T(8,128)(2,1)} %param.12) | copy-start | bytes 9437188
  200.8 6.0 %copy-start.7 = (bf16[576,4096]{1,0:T(8,128)(2,1)S(1)}, bf16[576,4096]{1,0:T(8,128)(2,1)}, u32[]{:S(2)}) copy-start(bf16[576,4096]{1,0:T(8,128)(2,1)} %all-gather.5.cloned.1.call-done) | copy-start | bytes 14155780
  258.2 6.6 %copy-start.1 = (f32[576,384]{1,0:T(8,128)S(1)}, f32[576,384]{1,0:T(8,128)}, u32[]{:S(2)}) copy-start(f32[576,384]{1,0:T(8,128)} %fusion.2) | copy-start | bytes 2654212
  258.2 6.6 %copy-start.4 = (f32[576,384]{1,0:T(8,128)S(1)}, f32[576,384]{1,0:T(8,128)}, u32[]{:S(2)}) copy-start(f32[576,384]{1,0:T(8,128)} %fusion.5) | copy-start | bytes 2654212
  264.8 2.9 copy-start.3
  401.4 7.2 %copy-start.6 = (f32[64,64]{0,1:T(8,128)S(1)}, f32[64,64]{0,1:T(8,128)}, u32[]{:S(2)}) copy-start(f32[64,64]{0,1:T(8,128)} %copy-done.5) | copy-start | bytes 49156
Sparse Core Ops, SparseCore 0:
  150.2 50.5 all-gather.4
  202.6 55.5 all-gather.2
  272.4 54.1 reduce-scatter.1

commit v2 on v1

v2 whole, which is shorter than its diff:
```python
import jax
import jax.numpy as jnp
from jax import lax
from jax.experimental import pallas as pl
from jax.experimental.pallas import tpu as pltpu
from jax.sharding import PartitionSpec as P

NZ, NY, NC, NX = 8, 4, 2, 4
TOP = 8
CAP = 9
ROWS = 64
SLOTS = NZ * NC
CH = SLOTS * CAP
W = 1024
HALF = W // 2
FH = 384
META = 128
ORDER = (0, 1, 3, 2)
MESH = pl.DeviceIdType.MESH
F32 = jnp.float32
BF = jnp.bfloat16
NT = (((1,), (1,)), ((), ()))


def dot(a, b):
    return jnp.dot(a, b, preferred_element_type=F32)


def dot_nt(a, b):
    return lax.dot_general(a, b, NT, preferred_element_type=F32)


def iota(shape, dim):
    return lax.broadcasted_iota(jnp.int32, shape, dim)


def kernel(
    tok_ref, grd_ref, ids_ref, rw_ref, wg_ref, wu_ref, wd_ref,
    gt_ref, gw_ref,
    xt, xg, pick, put, st, sg, rt, rg, rtx, rgx, wgu, wdv, gu, dd, ha, hb, fl, fr,
    vv, qq, yy, tw, bb, ff, gx, gv, gq, gl, ga, code_ref,
    w_sem, zrt, zrg, zst, zsg, yrt, yrg, yst, ysg, xrt, xrg, xst, xsg,
    cxr, cxs, gxr, gxs, cyr, cys, gyr, gys, twr, tws, zcr, zcs, gzr, gzs,
):
    me = lax.axis_index("expert")
    x = lax.axis_index("tensor")
    z = me // (NY * NC)
    y = (me // NC) % NY
    c = me % NC

    def dev(dz=0, dy=0, dc=0, dx=0):
        e = (((z + dz) % NZ) * NY + (y + dy) % NY) * NC + (c + dc) % NC
        return (e, (x + dx) % NX)

    def remote(src, dst, ssem, rsem, where):
        return pltpu.make_async_remote_copy(
            src_ref=src, dst_ref=dst, send_sem=ssem, recv_sem=rsem,
            device_id=where, device_id_type=MESH,
        )

    sends = []

    def send(*args):
        copy = remote(*args)
        copy.start()
        sends.append(copy)

    def arrived(dst, rsem):
        remote(dst, dst, rsem, rsem, dev(dz=1)).wait_recv()

    loads = []
    for r in range(NX):
        at = pl.multiple_of(((x + r) % NX) * W, W)
        loads.append(pltpu.make_async_copy(
            wg_ref.at[0, pl.ds(at, W), :], wgu.at[r, :, 0:FH], w_sem.at[3 * r]))
        loads.append(pltpu.make_async_copy(
            wu_ref.at[0, pl.ds(at, W), :], wgu.at[r, :, FH:2 * FH], w_sem.at[3 * r + 1]))
        loads.append(pltpu.make_async_copy(
            wd_ref.at[0, :, pl.ds(at, W)], wdv.at[r], w_sem.at[3 * r + 2]))
    for load in loads:
        load.start()

    barrier = pltpu.get_barrier_semaphore()
    partners = [dev(dz=d, dc=k) for d in range(NZ) for k in range(NC) if d or k]
    partners += [dev(dy=d) for d in range(1, NY)] + [dev(dx=d) for d in range(1, NX)]
    for partner in partners:
        pl.semaphore_signal(barrier, inc=1, device_id=partner, device_id_type=MESH)

    lane = iota((ROWS, META), 1)
    named = jnp.zeros((ROWS, META), F32)
    weight = jnp.zeros((ROWS, META), F32)
    for k in range(TOP):
        idk = ids_ref[:, k:k + 1]
        named = named + jnp.where(lane == idk, 1.0, 0.0)
        weight = weight + jnp.where(lane == idk + 64, rw_ref[:, k:k + 1], 0.0)
    below = (iota((ROWS, ROWS), 0) > iota((ROWS, ROWS), 1)).astype(F32).astype(BF)
    code = named * (dot(below, named.astype(BF)) + 1.0)
    code_ref[...] = code
    xt[0, :, 0:W] = tok_ref[...]
    xt[0, :, W:W + META] = (code + weight).astype(BF)
    xg[0] = grd_ref[...]
    gx[...] = jnp.zeros_like(gx)

    pl.semaphore_wait(barrier, len(partners))

    def ring(buf, slot, rsem, ssem):
        if slot == 0:
            send(buf.at[0], buf.at[7], ssem.at[0], rsem.at[7], dev(dz=1))
            send(buf.at[0], buf.at[1], ssem.at[8], rsem.at[1], dev(dz=NZ - 1))
        elif slot > 4:
            send(buf.at[slot], buf.at[slot - 1], ssem.at[slot], rsem.at[slot - 1], dev(dz=1))
        elif slot < 3:
            send(
                buf.at[slot], buf.at[slot + 1], ssem.at[slot], rsem.at[slot + 1], dev(dz=NZ - 1)
            )
        send(buf.at[slot], buf.at[slot + 8], ssem.at[slot + 9], rsem.at[slot + 8], dev(dc=1))

    def step(buf, s, rsem, ssem):
        for slot in ((8 - s, s) if s < 4 else (4,)):
            arrived(buf.at[slot], rsem.at[slot])
            ring(buf, slot, rsem, ssem)

    tok_z = (zrt, zst)
    grd_z = (zrg, zsg)
    ring(xt, 0, *tok_z)
    step(xt, 1, *tok_z)
    ring(xg, 0, *grd_z)
    step(xt, 2, *tok_z)
    step(xg, 1, *grd_z)
    step(xt, 3, *tok_z)
    step(xg, 2, *grd_z)
    step(xt, 4, *tok_z)
    for slot in range(8, 16):
        arrived(xt.at[slot], zrt.at[slot])

    tokens = SLOTS * ROWS
    meta = xt[:, :, W:W + META].reshape(tokens, META)
    for g in range(NY):
        e = (z * NY + (y + g) % NY) * NC + c
        choose = (iota((CH, META), 1) == e).astype(F32).astype(BF)
        got = dot_nt(choose, meta)
        row, col = iota((CH, tokens), 0), iota((CH, tokens), 1)
        hit = (got == (row % CAP + 1).astype(F32)) & (row // CAP == col // ROWS)
        pick[g * CH:(g + 1) * CH, :] = jnp.where(hit, 1.0, 0.0).astype(BF)

    def gather(buf, width, own, out, rows):
        data = buf[...].reshape(tokens, width)
        own[0] = dot(pick[0:CH, :], data).astype(BF)
        rows()
        rest = dot(pick[CH:NY * CH, :], data).astype(BF)
        out[...] = rest.reshape(NY - 1, CH, width)

    def x_first(o, own, ext, ssem, rsem):
        send(own.at[o, :, 0:W], ext.at[2, o], ssem.at[o, 0], rsem.at[o, 0], dev(dx=1))
        send(own.at[o, :, 0:W], ext.at[0, o], ssem.at[o, 1], rsem.at[o, 1], dev(dx=NX - 1))

    def x_second(o, ext, ssem, rsem):
        arrived(ext.at[2, o], rsem.at[o, 0])
        send(ext.at[2, o, :, 0:HALF], ext.at[1, o, :, 0:HALF], ssem.at[o, 2], rsem.at[o, 2], dev(dx=1))
        arrived(ext.at[0, o], rsem.at[o, 1])
        send(
            ext.at[0, o, :, HALF:W], ext.at[1, o, :, HALF:W],
            ssem.at[o, 3], rsem.at[o, 3], dev(dx=NX - 1),
        )

    def x_third(o, ext, rsem):
        arrived(ext.at[1, o, :, 0:HALF], rsem.at[o, 2])
        arrived(ext.at[1, o, :, HALF:W], rsem.at[o, 3])

    def y_send(out, own, ssem, rsem):
        for g in (3, 1, 2):
            o = (NY - g) % NY
            send(out.at[g - 1], own.at[o], ssem.at[g], rsem.at[o], dev(dy=g))

    tok_x = (xst, xrt)
    grd_x = (xsg, xrg)
    step(xg, 3, *grd_z)
    gather(xt, W + META, rt, st, lambda: x_first(0, rt, rtx, *tok_x))
    y_send(st, rt, yst, yrt)
    step(xg, 4, *grd_z)
    for slot in range(8, 16):
        arrived(xg.at[slot], zrg.at[slot])
    gather(xg, W, rg, sg, lambda: None)
    y_send(sg, rg, ysg, yrg)
    for load in loads:
        load.wait()
    for j in range(1, NY):
        arrived(rt.at[ORDER[j]], yrt.at[ORDER[j]])
        x_first(ORDER[j], rt, rtx, *tok_x)
        x_second(ORDER[j - 1], rtx, *tok_x)
    x_first(0, rg, rgx, *grd_x)
    x_second(ORDER[3], rtx, *tok_x)

    def quarter(own, ext, o, r):
        return own[o, :, 0:W] if r == 0 else ext[r - 1, o]

    def forward(o):
        x_third(o, rtx, xrt)
        total = dot(quarter(rt, rtx, o, 0), wgu[0])
        for r in range(1, NX):
            total = total + dot(quarter(rt, rtx, o, r), wgu[r])
        gu[o] = total

    for j in range(NY):
        if j:
            arrived(rg.at[ORDER[j]], yrg.at[ORDER[j]])
            x_first(ORDER[j], rg, rgx, *grd_x)
            x_second(ORDER[j - 1], rgx, *grd_x)
        forward(ORDER[j])
    x_second(ORDER[3], rgx, *grd_x)

    ones = jnp.ones((8, FH), BF)

    def backward(o):
        x_third(o, rgx, xrg)
        back = dot_nt(quarter(rg, rgx, o, 0), wdv[0])
        for r in range(1, NX):
            back = back + dot_nt(quarter(rg, rgx, o, r), wdv[r])
        gate = gu[o, :, 0:FH]
        up = gu[o, :, FH:2 * FH]
        sig = 1.0 / (1.0 + jnp.exp(-gate))
        act = gate * sig
        prod = act * up * back
        high = prod.astype(BF)
        low = (prod - high.astype(F32)).astype(BF)
        gx[0, o, :, 0:CH] = dot_nt(ones, high) + dot_nt(ones, low)
        for k, d in enumerate((1, 3, 2)):
            send(gx.at[0, o], gx.at[NX - d, o], gxs.at[o, k], gxr.at[o, k], dev(dx=d))
        rows = rt[o, :, W:W + META].astype(F32)
        scale = jnp.sum(
            jnp.where(iota((CH, META), 1) == me + 64, rows, 0.0), axis=1, keepdims=True
        )
        scaled = scale * back
        dgate = (scaled * up * sig * (1.0 + gate * (1.0 - sig))).astype(BF)
        dup = (scaled * act).astype(BF)
        both = jnp.concatenate([dgate, dup], axis=1)
        dd[2, o] = dot_nt(both, wgu[2]).astype(BF)
        send(dd.at[2, o, :, 0:HALF], ha.at[o], cxs.at[o, 0], cxr.at[o, 0], dev(dx=1))
        send(dd.at[2, o, :, HALF:W], hb.at[o], cxs.at[o, 1], cxr.at[o, 1], dev(dx=NX - 1))
        for r in (1, 3, 0):
            dd[r, o] = dot_nt(both, wgu[r]).astype(BF)

    def sum_second(o):
        arrived(ha.at[o], cxr.at[o, 0])
        dd[1, o, :, 0:HALF] = (dd[1, o, :, 0:HALF].astype(F32) + ha[o].astype(F32)).astype(BF)
        send(dd.at[1, o], fl.at[o], cxs.at[o, 2], cxr.at[o, 2], dev(dx=1))
        arrived(hb.at[o], cxr.at[o, 1])
        dd[3, o, :, HALF:W] = (dd[3, o, :, HALF:W].astype(F32) + hb[o].astype(F32)).astype(BF)
        send(dd.at[3, o], fr.at[o], cxs.at[o, 3], cxr.at[o, 3], dev(dx=NX - 1))

    def sum_third(o):
        g = (NY - o) % NY
        for k, d in enumerate((1, 3, 2)):
            arrived(gx.at[NX - d, o], gxr.at[o, k])
        parts = (gx[0, o] + gx[1, o]) + (gx[2, o] + gx[3, o])
        arrived(fl.at[o], cxr.at[o, 2])
        arrived(fr.at[o], cxr.at[o, 3])
        total = dd[0, o].astype(F32) + fl[o].astype(F32) + fr[o].astype(F32)
        if o == 0:
            qq[0] = total.astype(BF)
            gq[0] = parts
        else:
            vv[o] = total.astype(BF)
            gv[o] = parts
            send(vv.at[o], qq.at[g], cys.at[o], cyr.at[g], dev(dy=o))
            send(gv.at[o], gq.at[g], gys.at[o], gyr.at[g], dev(dy=o))

    for j in range(NY):
        backward(ORDER[j])
        if j:
            sum_second(ORDER[j - 1])
        if j > 1:
            sum_third(ORDER[j - 2])
    sum_second(ORDER[3])
    sum_third(ORDER[2])

    for g in range(NY):
        e = (z * NY + (y + g) % NY) * NC + c
        choose = (iota((META, CH), 0) == e).astype(F32).astype(BF)
        got = dot(meta, choose)
        row, col = iota((tokens, CH), 1), iota((tokens, CH), 0)
        hit = (got == (row % CAP + 1).astype(F32)) & (row // CAP == col // ROWS)
        put[g] = jnp.where(hit, 1.0, 0.0).astype(BF)

    sum_third(ORDER[3])
    for g in range(1, NY):
        arrived(gq.at[g], gyr.at[g])
    rows8 = iota((8, 2 * META), 0)
    mine = jnp.zeros((8, 2 * META), F32)
    for g in range(NY):
        mine = mine + jnp.where(rows8 == g, gq[g], 0.0)
    gl[...] = mine
    ga[0] = mine
    for g in range(1, NY):
        arrived(qq.at[g], cyr.at[g])
    half = tokens // 2

    def spread(lo):
        total = dot(put[0, lo:lo + half, :], qq[0])
        for g in range(1, NY):
            total = total + dot(put[g, lo:lo + half, :], qq[g])
        return total

    yy[...] = spread(half).astype(BF).reshape(NZ, ROWS, W)
    send(yy, tw, tws.at[0], twr.at[0], dev(dc=1))
    for k in range(NC):
        for d in range(NZ):
            if d or k:
                slot = k * 8 + d
                back_slot = k * 8 + (NZ - d) % NZ
                send(gl, ga.at[back_slot], gzs.at[slot], gzr.at[back_slot], dev(dz=d, dc=k))
    own = spread(0)
    arrived(tw, twr.at[0])
    own = own.reshape(NZ, ROWS, W) + tw[...].astype(F32)
    bb[...] = own.astype(BF)
    for d in (4, 3, 5, 2, 6, 1, 7):
        send(bb.at[d], ff.at[(NZ - d) % NZ], zcs.at[d], zcr.at[(NZ - d) % NZ], dev(dz=d))

    for slot in range(1, SLOTS):
        arrived(ga.at[slot], gzr.at[slot])
    table = ga[...].reshape(SLOTS * 8, 2 * META)
    high = table.astype(BF)
    low = (table - high.astype(F32)).astype(BF)
    code = code_ref[...]
    lane8 = iota((ROWS, TOP), 1)
    result = jnp.zeros((ROWS, TOP), F32)
    for k in range(TOP):
        idk = ids_ref[:, k:k + 1]
        place = jnp.sum(jnp.where(lane == idk, code, 0.0), axis=1, keepdims=True)
        dz = ((idk >> 3) - z) & 7
        dy = ((idk >> 1) - y) & 3
        dc = (idk - c) & 1
        wanted = (dc * 8 + dz) * 8 + dy
        line = (dc * 8 + ((8 - dz) & 7)) * CAP
        onehot = (lane == wanted).astype(F32).astype(BF)
        values = dot(onehot, high) + dot(onehot, low)
        at = iota((ROWS, 2 * META), 1) - line + 1
        value = jnp.sum(jnp.where(at.astype(F32) == place, values, 0.0), axis=1, keepdims=True)
        result = result + jnp.where(lane8 == k, value, 0.0)
    gw_ref[...] = result.astype(BF)

    total = bb[0].astype(F32)
    for d in range(1, NZ):
        arrived(ff.at[d], zcr.at[d])
        total = total + ff[d].astype(F32)
    gt_ref[...] = total.astype(BF)
    for copy in sends:
        copy.wait_send()


def body(tokens, grad_out, expert_ids, route_weights, gate_weights, up_weights, down_weights):
    vmem = pl.BlockSpec(memory_space=pltpu.VMEM)
    hbm = pl.BlockSpec(memory_space=pl.ANY)
    V = pltpu.VMEM
    D = pltpu.SemaphoreType.DMA
    n_tok = SLOTS * ROWS
    scratch = [
        V((SLOTS, ROWS, W + META), BF), V((SLOTS, ROWS, W), BF),
        V((NY * CH, n_tok), BF), V((NY, n_tok, CH), BF),
        V((NY - 1, CH, W + META), BF), V((NY - 1, CH, W), BF),
        V((NY, CH, W + META), BF), V((NY, CH, W), BF),
        V((NX - 1, NY, CH, W), BF), V((NX - 1, NY, CH, W), BF),
        V((NX, W, 2 * FH), BF), V((NX, FH, W), BF),
        V((NY, CH, 2 * FH), F32), V((NX, NY, CH, W), BF),
        V((NY, CH, HALF), BF), V((NY, CH, HALF), BF), V((NY, CH, W), BF), V((NY, CH, W), BF),
        V((NY, CH, W), BF), V((NY, CH, W), BF),
        V((NZ, ROWS, W), BF), V((NZ, ROWS, W), BF), V((NZ, ROWS, W), BF), V((NZ, ROWS, W), BF),
        V((NX, NY, 8, 2 * META), F32), V((NY, 8, 2 * META), F32), V((NY, 8, 2 * META), F32),
        V((8, 2 * META), F32), V((SLOTS, 8, 2 * META), F32), V((ROWS, META), F32),
        D((12,)),
        D((16,)), D((16,)), D((17,)), D((17,)),
        D((4,)), D((4,)), D((4,)), D((4,)),
        D((4, 4)), D((4, 4)), D((4, 4)), D((4, 4)),
        D((4, 4)), D((4, 4)), D((4, 3)), D((4, 3)),
        D((4,)), D((4,)), D((4,)), D((4,)),
        D((1,)), D((1,)), D((8,)), D((8,)), D((16,)), D((16,)),
    ]
    return pl.pallas_call(
        kernel,
        out_shape=(
            jax.ShapeDtypeStruct(tokens.shape, BF),
            jax.ShapeDtypeStruct(expert_ids.shape, BF),
        ),
        in_specs=[vmem, vmem, vmem, vmem, hbm, hbm, hbm],
        out_specs=(vmem, vmem),
        scratch_shapes=scratch,
        compiler_params=pltpu.CompilerParams(
            collective_id=0, has_side_effects=True, vmem_limit_bytes=66 * 1000 * 1000
        ),
    )(
        tokens, grad_out, expert_ids, route_weights.astype(F32),
        gate_weights, up_weights, down_weights,
    )


def solution(mesh):
    in_specs = (
        P("expert", "tensor"),
        P("expert", "tensor"),
        P("expert", None),
        P("expert", None),
        P("expert", None, "tensor"),
        P("expert", None, "tensor"),
        P("expert", "tensor", None),
    )
    out_specs = (P("expert", "tensor"), P("expert", None))
    return jax.shard_map(body, mesh=mesh, in_specs=in_specs, out_specs=out_specs, check_vma=False)
```

time: 417 us -> 206 us (0.49)
  Pallas kernels: 0 us -> 200 us
  blocking collectives: 192 us -> 0 us
  waiting for transfers between devices: 145 us -> 0 us
  matrix products: 27.7 us -> 0 us
  local copies, waits for them, and re-layouts: 29.4 us -> 5.69 us
  between operations: 13.9 us -> 0.64 us
  other arithmetic: 8.48 us -> 0 us
    pallas_call x0 -> x1, Pallas kernels: none -> 200 us  [body(): pl.pallas_call(kernel, out_shape=(jax.ShapeDtypeStruct(tokens.shape, BF),...]
    all_to_all x2 -> x0, blocking collectives: 185 us -> none  [the longest x1 116 us: body(): lax.all_to_all(sent, 'expert', split_axis=0, concat_axis=0, tiled=True)]
    all_gather x2 -> x0, waiting for transfers between devices: 96.6 us -> none  [the longest x1 48.7 us: body(): got_tokens = lax.all_gather(got[:, :width], 'tensor', axis=1, tiled=True)]
    reduce_scatter x1 -> x0, waiting for transfers between devices: 47.6 us -> none  [body(): lax.psum_scatter(grad_rows, 'tensor', scatter_dimension=1, tiled=True)]
    dot_general x8 -> x0, matrix products: 27.7 us -> none  [the longest x1 6.59 us: expert_rows(): lax.dot_general(grads, down_weight, contract, preferred_element_type=jnp....]
    all_to_all x4 -> x0, local copies, waits for them, and re-layouts: 16.6 us -> none  [the longest x2 9.46 us: body(): lax.all_to_all(sent, 'expert', split_axis=0, concat_axis=0, tiled=True)]
    psum x1 -> x0, blocking collectives: 6.71 us -> none  [body(): weight_total = lax.psum(weight_rows, 'tensor').astype(jnp.bfloat16)]
    concatenate x2 -> x0, other arithmetic: 4.18 us -> none  [the longest x1 2.45 us: body(): jnp.concatenate([summed, tail], axis=1)]
  transfers between devices with their start and end apart: 3 -> 0, of which waited for: 3 -> 0; matrix products, arithmetic and copies ran while one was open for 3% -> 0% of each run, Pallas kernels for 0% -> 0%
where the time goes in v2:
time: 206 us
  Pallas kernels  200 us (97%)
  local copies, waits for them, and re-layouts  5.69 us (3%)
    pallas_call x1, Pallas kernels, body(): pl.pallas_call(kernel, out_shape=(jax.ShapeDtypeStruct(tokens.shape, BF),...  200 us

profile of v2, /device:TPU:1, one launch (start us, length us, event | category | flops | bytes accessed | tf_op | source)
XLA Modules:
  0.0 205.8 jit_solution(10906294730049243871)
XLA Ops:
  0.6 1.4 copy.12.ids_ref
  2.0 1.4 copy.13.rw_ref
  3.4 199.5 %shard_map.86 = (bf16[64,1024]{1,0:T(8,128)(2,1)}, bf16[64,8]{1,0:T(8,128)(2,1)}) custom-call(bf16[64,1024]{1,0:T(8,128)(2,1)} %tok_ref.1, bf16[64,1024]{1,0:T(8,128)(2,1)} %grd_ref.1, s32[64,8]{1,0:T(8,128)} %copy.12.ids_ref, f32[64,8]{1,0:T(8,128)} %copy.13.rw_ref, bf16[1,4096,384]{2,1,0:T(8,128)(2,1)} %wg_ref.1, bf16[1,4096,384]{2,1,0:T(8,128)(2,1)} %wu_ref.1, ...), custom_call_target="tpu_custom_call" | custom-call | tf_op jit(solution)/shard_map/pallas_call | solution.py:378
  202.9 1.4 copy.14
  204.3 1.6 copy.16

commit v3 on v2

--- a/solution.py
+++ b/solution.py
@@ -16,6 +16,7 @@
 FH = 384
 META = 128
 ORDER = (0, 1, 3, 2)
+BACK = (1, 2, 3, 0)
 MESH = pl.DeviceIdType.MESH
 F32 = jnp.float32
 BF = jnp.bfloat16
@@ -38,7 +39,7 @@
     tok_ref, grd_ref, ids_ref, rw_ref, wg_ref, wu_ref, wd_ref,
     gt_ref, gw_ref,
     xt, xg, pick, put, st, sg, rt, rg, rtx, rgx, wgu, wdv, gu, dd, ha, hb, fl, fr,
-    vv, qq, yy, tw, bb, ff, gx, gv, gq, gl, ga, code_ref,
+    vv, qq, yy, tw, bb, ff, gx, gv, gq, gl, ga, code_ref, acc,
     w_sem, zrt, zrg, zst, zsg, yrt, yrg, yst, ysg, xrt, xrg, xst, xsg,
     cxr, cxs, gxr, gxs, cyr, cys, gyr, gys, twr, tws, zcr, zcs, gzr, gzs,
 ):
@@ -167,8 +168,8 @@
         arrived(ext.at[1, o, :, 0:HALF], rsem.at[o, 2])
         arrived(ext.at[1, o, :, HALF:W], rsem.at[o, 3])
 
-    def y_send(out, own, ssem, rsem):
-        for g in (3, 1, 2):
+    def y_send(out, own, order, ssem, rsem):
+        for g in order:
             o = (NY - g) % NY
             send(out.at[g - 1], own.at[o], ssem.at[g], rsem.at[o], dev(dy=g))
 
@@ -176,19 +177,20 @@
     grd_x = (xsg, xrg)
     step(xg, 3, *grd_z)
     gather(xt, W + META, rt, st, lambda: x_first(0, rt, rtx, *tok_x))
-    y_send(st, rt, yst, yrt)
+    y_send(st, rt, (3, 1, 2), yst, yrt)
     step(xg, 4, *grd_z)
     for slot in range(8, 16):
         arrived(xg.at[slot], zrg.at[slot])
     gather(xg, W, rg, sg, lambda: None)
-    y_send(sg, rg, ysg, yrg)
+    y_send(sg, rg, (3, 2, 1), ysg, yrg)
     for load in loads:
         load.wait()
     for j in range(1, NY):
         arrived(rt.at[ORDER[j]], yrt.at[ORDER[j]])
         x_first(ORDER[j], rt, rtx, *tok_x)
         x_second(ORDER[j - 1], rtx, *tok_x)
-    x_first(0, rg, rgx, *grd_x)
+    arrived(rg.at[BACK[0]], yrg.at[BACK[0]])
+    x_first(BACK[0], rg, rgx, *grd_x)
     x_second(ORDER[3], rtx, *tok_x)
 
     def quarter(own, ext, o, r):
@@ -203,11 +205,12 @@
 
     for j in range(NY):
         if j:
-            arrived(rg.at[ORDER[j]], yrg.at[ORDER[j]])
-            x_first(ORDER[j], rg, rgx, *grd_x)
-            x_second(ORDER[j - 1], rgx, *grd_x)
+            if BACK[j]:
+                arrived(rg.at[BACK[j]], yrg.at[BACK[j]])
+            x_first(BACK[j], rg, rgx, *grd_x)
+            x_second(BACK[j - 1], rgx, *grd_x)
         forward(ORDER[j])
-    x_second(ORDER[3], rgx, *grd_x)
+    x_second(BACK[3], rgx, *grd_x)
 
     ones = jnp.ones((8, FH), BF)
 
@@ -266,13 +269,13 @@
             send(gv.at[o], gq.at[g], gys.at[o], gyr.at[g], dev(dy=o))
 
     for j in range(NY):
-        backward(ORDER[j])
+        backward(BACK[j])
         if j:
-            sum_second(ORDER[j - 1])
+            sum_second(BACK[j - 1])
         if j > 1:
-            sum_third(ORDER[j - 2])
-    sum_second(ORDER[3])
-    sum_third(ORDER[2])
+            sum_third(BACK[j - 2])
+    sum_second(BACK[3])
+    sum_third(BACK[2])
 
     for g in range(NY):
         e = (z * NY + (y + g) % NY) * NC + c
@@ -282,39 +285,83 @@
         hit = (got == (row % CAP + 1).astype(F32)) & (row // CAP == col // ROWS)
         put[g] = jnp.where(hit, 1.0, 0.0).astype(BF)
 
-    sum_third(ORDER[3])
+    for n, g in enumerate((3, 2, 1)):
+        arrived(qq.at[g], cyr.at[g])
+        part = dot(put[g], qq[g]).reshape(SLOTS, ROWS, W)
+        acc[...] = part if n == 0 else acc[...] + part
     for g in range(1, NY):
         arrived(gq.at[g], gyr.at[g])
+
+    sum_third(BACK[3])
+
+    def spread(lo, hi):
+        own = dot(put[0, lo * ROWS:hi * ROWS, :], qq[0])
+        return acc[lo:hi] + own.reshape(hi - lo, ROWS, W)
+
+    pieces = ((3, 6), (6, 8), (0, 3))
+    far = ((4, 3, 5), (6, 7), (2, 1, 0))
+    for (lo, hi), ds in zip(pieces, far):
+        yy[lo:hi] = spread(NZ + lo, NZ + hi).astype(BF)
+        for d in ds:
+            send(yy.at[d], tw.at[d], tws.at[d], twr.at[d], dev(dc=1))
+
+    def twin_sum(d):
+        arrived(tw.at[d], twr.at[d])
+        bb[d] = (acc[d] + tw[d].astype(F32)).astype(BF)
+
+    def z_send(way, h, r):
+        at = slice(h * HALF, (h + 1) * HALF)
+        d = NZ - r - 1 if way else r + 1
+        send(
+            bb.at[d, :, at], ff.at[4 * way + r, :, at], zcs.at[way, h, r], zcr.at[way, h, r],
+            dev(dz=NZ - 1 if way else 1),
+        )
+
+    def z_step(way, h, r):
+        at = slice(h * HALF, (h + 1) * HALF)
+        d = NZ - r if way else r
+        arrived(ff.at[4 * way + r, :, at], zcr.at[way, h, r])
+        bb[d, :, at] = (bb[d, :, at].astype(F32) + ff[4 * way + r, :, at].astype(F32)).astype(BF)
+        z_send(way, h, r - 1)
+
+    acc[3:6] = spread(3, 6)
+    twin_sum(4)
+    z_send(0, 0, 3)
+    z_send(1, 1, 3)
+    twin_sum(3)
+    z_send(0, 1, 2)
+    twin_sum(5)
+    z_send(1, 0, 2)
+    acc[6:8] = spread(6, 8)
+    acc[0:3] = spread(0, 3)
+
     rows8 = iota((8, 2 * META), 0)
     mine = jnp.zeros((8, 2 * META), F32)
     for g in range(NY):
         mine = mine + jnp.where(rows8 == g, gq[g], 0.0)
     gl[...] = mine
     ga[0] = mine
-    for g in range(1, NY):
-        arrived(qq.at[g], cyr.at[g])
-    half = tokens // 2
-
-    def spread(lo):
-        total = dot(put[0, lo:lo + half, :], qq[0])
-        for g in range(1, NY):
-            total = total + dot(put[g, lo:lo + half, :], qq[g])
-        return total
-
-    yy[...] = spread(half).astype(BF).reshape(NZ, ROWS, W)
-    send(yy, tw, tws.at[0], twr.at[0], dev(dc=1))
     for k in range(NC):
         for d in range(NZ):
             if d or k:
                 slot = k * 8 + d
                 back_slot = k * 8 + (NZ - d) % NZ
                 send(gl, ga.at[back_slot], gzs.at[slot], gzr.at[back_slot], dev(dz=d, dc=k))
-    own = spread(0)
-    arrived(tw, twr.at[0])
-    own = own.reshape(NZ, ROWS, W) + tw[...].astype(F32)
-    bb[...] = own.astype(BF)
-    for d in (4, 3, 5, 2, 6, 1, 7):
-        send(bb.at[d], ff.at[(NZ - d) % NZ], zcs.at[d], zcr.at[(NZ - d) % NZ], dev(dz=d))
+
+    z_step(0, 0, 3)
+    z_step(1, 1, 3)
+    twin_sum(2)
+    z_step(0, 1, 2)
+    twin_sum(6)
+    z_step(1, 0, 2)
+    z_step(0, 0, 2)
+    z_step(1, 1, 2)
+    twin_sum(1)
+    z_step(0, 1, 1)
+    twin_sum(7)
+    z_step(1, 0, 1)
+    z_step(0, 0, 1)
+    z_step(1, 1, 1)
 
     for slot in range(1, SLOTS):
         arrived(ga.at[slot], gzr.at[slot])
@@ -339,11 +386,14 @@
         result = result + jnp.where(lane8 == k, value, 0.0)
     gw_ref[...] = result.astype(BF)
 
-    total = bb[0].astype(F32)
-    for d in range(1, NZ):
-        arrived(ff.at[d], zcr.at[d])
-        total = total + ff[d].astype(F32)
-    gt_ref[...] = total.astype(BF)
+    arrived(tw.at[0], twr.at[0])
+    total = acc[0] + tw[0].astype(F32)
+    for h in range(2):
+        at = slice(h * HALF, (h + 1) * HALF)
+        for way in range(2):
+            arrived(ff.at[4 * way, :, at], zcr.at[way, h, 0])
+        near = ff[0, :, at].astype(F32) + ff[4, :, at].astype(F32)
+        gt_ref[:, at] = (total[:, at] + near).astype(BF)
     for copy in sends:
         copy.wait_send()
 
@@ -367,13 +417,14 @@
         V((NZ, ROWS, W), BF), V((NZ, ROWS, W), BF), V((NZ, ROWS, W), BF), V((NZ, ROWS, W), BF),
         V((NX, NY, 8, 2 * META), F32), V((NY, 8, 2 * META), F32), V((NY, 8, 2 * META), F32),
         V((8, 2 * META), F32), V((SLOTS, 8, 2 * META), F32), V((ROWS, META), F32),
+        V((SLOTS, ROWS, W), F32),
         D((12,)),
         D((16,)), D((16,)), D((17,)), D((17,)),
         D((4,)), D((4,)), D((4,)), D((4,)),
         D((4, 4)), D((4, 4)), D((4, 4)), D((4, 4)),
         D((4, 4)), D((4, 4)), D((4, 3)), D((4, 3)),
         D((4,)), D((4,)), D((4,)), D((4,)),
-        D((1,)), D((1,)), D((8,)), D((8,)), D((16,)), D((16,)),
+        D((8,)), D((8,)), D((2, 2, 4)), D((2, 2, 4)), D((16,)), D((16,)),
     ]
     return pl.pallas_call(
         kernel,

time: 206 us -> 189 us (0.917)
  Pallas kernels: 200 us -> 180 us
    pallas_call x1, Pallas kernels: 200 us -> 180 us  [body(): pl.pallas_call(kernel, out_shape=(jax.ShapeDtypeStruct(tokens.shape, BF),...]
where the time goes in v3:
time: 189 us; the launch traced here: 187 us
  Pallas kernels  180 us (95%)
  local copies, waits for them, and re-layouts  5.69 us (3%)
    pallas_call x1, Pallas kernels, body(): pl.pallas_call(kernel, out_shape=(jax.ShapeDtypeStruct(tokens.shape, BF),...  180 us

profile of v3, /device:TPU:1, one launch (start us, length us, event | category | flops | bytes accessed | tf_op | source)
XLA Modules:
  0.0 186.8 jit_solution(6296083478510394481)
XLA Ops:
  0.6 1.4 copy.12.ids_ref
  2.0 1.4 copy.13.rw_ref
  3.4 180.5 %shard_map.86 = (bf16[64,1024]{1,0:T(8,128)(2,1)}, bf16[64,8]{1,0:T(8,128)(2,1)}) custom-call(bf16[64,1024]{1,0:T(8,128)(2,1)} %tok_ref.1, bf16[64,1024]{1,0:T(8,128)(2,1)} %grd_ref.1, s32[64,8]{1,0:T(8,128)} %copy.12.ids_ref, f32[64,8]{1,0:T(8,128)} %copy.13.rw_ref, bf16[1,4096,384]{2,1,0:T(8,128)(2,1)} %wg_ref.1, bf16[1,4096,384]{2,1,0:T(8,128)(2,1)} %wu_ref.1, ...), custom_call_target="tpu_custom_call" | custom-call | tf_op jit(solution)/shard_map/pallas_call | solution.py:429
  183.9 1.4 copy.14
  185.2 1.6 copy.16

commit v4 on v3

--- a/solution.py
+++ b/solution.py
@@ -41,7 +41,7 @@
     xt, xg, pick, put, st, sg, rt, rg, rtx, rgx, wgu, wdv, gu, dd, ha, hb, fl, fr,
     vv, qq, yy, tw, bb, ff, gx, gv, gq, gl, ga, code_ref, acc,
     w_sem, zrt, zrg, zst, zsg, yrt, yrg, yst, ysg, xrt, xrg, xst, xsg,
-    cxr, cxs, gxr, gxs, cyr, cys, gyr, gys, twr, tws, zcr, zcs, gzr, gzs,
+    cxr, cxs, gxr, gxs, cyr, cys, gyr, gys, twr, tws, zcr, zcs, gzr, gzs, opr, ops,
 ):
     me = lax.axis_index("expert")
     x = lax.axis_index("tensor")
@@ -99,7 +99,7 @@
     code_ref[...] = code
     xt[0, :, 0:W] = tok_ref[...]
     xt[0, :, W:W + META] = (code + weight).astype(BF)
-    xg[0] = grd_ref[...]
+    xg[0, :, 0:W] = grd_ref[...]
     gx[...] = jnp.zeros_like(gx)
 
     pl.semaphore_wait(barrier, len(partners))
@@ -124,12 +124,11 @@
     tok_z = (zrt, zst)
     grd_z = (zrg, zsg)
     ring(xt, 0, *tok_z)
-    step(xt, 1, *tok_z)
+    send(grd_ref, xg.at[0, :, W:2 * W], ops.at[0], opr.at[0], dev(dx=2))
+    for n in range(1, 4):
+        step(xt, n, *tok_z)
+    arrived(xg.at[0, :, W:2 * W], opr.at[0])
     ring(xg, 0, *grd_z)
-    step(xt, 2, *tok_z)
-    step(xg, 1, *grd_z)
-    step(xt, 3, *tok_z)
-    step(xg, 2, *grd_z)
     step(xt, 4, *tok_z)
     for slot in range(8, 16):
         arrived(xt.at[slot], zrt.at[slot])
@@ -151,74 +150,84 @@
         rest = dot(pick[CH:NY * CH, :], data).astype(BF)
         out[...] = rest.reshape(NY - 1, CH, width)
 
-    def x_first(o, own, ext, ssem, rsem):
-        send(own.at[o, :, 0:W], ext.at[2, o], ssem.at[o, 0], rsem.at[o, 0], dev(dx=1))
-        send(own.at[o, :, 0:W], ext.at[0, o], ssem.at[o, 1], rsem.at[o, 1], dev(dx=NX - 1))
-
-    def x_second(o, ext, ssem, rsem):
-        arrived(ext.at[2, o], rsem.at[o, 0])
-        send(ext.at[2, o, :, 0:HALF], ext.at[1, o, :, 0:HALF], ssem.at[o, 2], rsem.at[o, 2], dev(dx=1))
-        arrived(ext.at[0, o], rsem.at[o, 1])
-        send(
-            ext.at[0, o, :, HALF:W], ext.at[1, o, :, HALF:W],
-            ssem.at[o, 3], rsem.at[o, 3], dev(dx=NX - 1),
-        )
-
-    def x_third(o, ext, rsem):
-        arrived(ext.at[1, o, :, 0:HALF], rsem.at[o, 2])
-        arrived(ext.at[1, o, :, HALF:W], rsem.at[o, 3])
+    def x_first(o):
+        for n, lo in enumerate((0, HALF)):
+            a, b = slice(lo, lo + HALF), slice(HALF - lo, W - lo)
+            send(
+                rt.at[o, :, a], rtx.at[2, o, :, a], xst.at[o, 2 * n], xrt.at[o, 2 * n], dev(dx=1)
+            )
+            send(
+                rt.at[o, :, b], rtx.at[0, o, :, b],
+                xst.at[o, 2 * n + 1], xrt.at[o, 2 * n + 1], dev(dx=NX - 1),
+            )
+
+    def x_second(o):
+        a, b = slice(0, HALF), slice(HALF, W)
+        arrived(rtx.at[2, o, :, a], xrt.at[o, 0])
+        send(rtx.at[2, o, :, a], rtx.at[1, o, :, a], xst.at[o, 4], xrt.at[o, 4], dev(dx=1))
+        arrived(rtx.at[0, o, :, b], xrt.at[o, 1])
+        send(rtx.at[0, o, :, b], rtx.at[1, o, :, b], xst.at[o, 5], xrt.at[o, 5], dev(dx=NX - 1))
+
+    def x_third(o):
+        a, b = slice(0, HALF), slice(HALF, W)
+        arrived(rtx.at[2, o, :, b], xrt.at[o, 2])
+        arrived(rtx.at[0, o, :, a], xrt.at[o, 3])
+        arrived(rtx.at[1, o, :, a], xrt.at[o, 4])
+        arrived(rtx.at[1, o, :, b], xrt.at[o, 5])
+
+    def x_grad(o):
+        send(rg.at[o, :, 0:W], rgx.at[1, o], xsg.at[o, 0], xrg.at[o, 0], dev(dx=1))
+        send(rg.at[o, :, 0:W], rgx.at[0, o], xsg.at[o, 1], xrg.at[o, 1], dev(dx=NX - 1))
 
     def y_send(out, own, order, ssem, rsem):
         for g in order:
             o = (NY - g) % NY
             send(out.at[g - 1], own.at[o], ssem.at[g], rsem.at[o], dev(dy=g))
 
-    tok_x = (xst, xrt)
-    grd_x = (xsg, xrg)
-    step(xg, 3, *grd_z)
-    gather(xt, W + META, rt, st, lambda: x_first(0, rt, rtx, *tok_x))
+    gather(xt, W + META, rt, st, lambda: x_first(0))
     y_send(st, rt, (3, 1, 2), yst, yrt)
+    for j in range(1, NY):
+        step(xg, j, *grd_z)
+        arrived(rt.at[ORDER[j]], yrt.at[ORDER[j]])
+        x_first(ORDER[j])
+        x_second(ORDER[j - 1])
     step(xg, 4, *grd_z)
     for slot in range(8, 16):
         arrived(xg.at[slot], zrg.at[slot])
-    gather(xg, W, rg, sg, lambda: None)
+    gather(xg, 2 * W, rg, sg, lambda: None)
     y_send(sg, rg, (3, 2, 1), ysg, yrg)
+    x_grad(0)
+    x_second(ORDER[3])
     for load in loads:
         load.wait()
-    for j in range(1, NY):
-        arrived(rt.at[ORDER[j]], yrt.at[ORDER[j]])
-        x_first(ORDER[j], rt, rtx, *tok_x)
-        x_second(ORDER[j - 1], rtx, *tok_x)
-    arrived(rg.at[BACK[0]], yrg.at[BACK[0]])
-    x_first(BACK[0], rg, rgx, *grd_x)
-    x_second(ORDER[3], rtx, *tok_x)
-
-    def quarter(own, ext, o, r):
-        return own[o, :, 0:W] if r == 0 else ext[r - 1, o]
+
+    def token_quarter(o, r):
+        return rt[o, :, 0:W] if r == 0 else rtx[r - 1, o]
+
+    def grad_quarter(o, r):
+        return rg[o, :, r // 2 * W:(r // 2 + 1) * W] if r % 2 == 0 else rgx[r // 2, o]
 
     def forward(o):
-        x_third(o, rtx, xrt)
-        total = dot(quarter(rt, rtx, o, 0), wgu[0])
+        x_third(o)
+        total = dot(token_quarter(o, 0), wgu[0])
         for r in range(1, NX):
-            total = total + dot(quarter(rt, rtx, o, r), wgu[r])
+            total = total + dot(token_quarter(o, r), wgu[r])
         gu[o] = total
 
     for j in range(NY):
-        if j:
-            if BACK[j]:
-                arrived(rg.at[BACK[j]], yrg.at[BACK[j]])
-            x_first(BACK[j], rg, rgx, *grd_x)
-            x_second(BACK[j - 1], rgx, *grd_x)
+        if j == NY - 1:
+            arrived(rg.at[BACK[0]], yrg.at[BACK[0]])
+            x_grad(BACK[0])
         forward(ORDER[j])
-    x_second(BACK[3], rgx, *grd_x)
 
     ones = jnp.ones((8, FH), BF)
 
     def backward(o):
-        x_third(o, rgx, xrg)
-        back = dot_nt(quarter(rg, rgx, o, 0), wdv[0])
+        arrived(rgx.at[1, o], xrg.at[o, 0])
+        arrived(rgx.at[0, o], xrg.at[o, 1])
+        back = dot_nt(grad_quarter(o, 0), wdv[0])
         for r in range(1, NX):
-            back = back + dot_nt(quarter(rg, rgx, o, r), wdv[r])
+            back = back + dot_nt(grad_quarter(o, r), wdv[r])
         gate = gu[o, :, 0:FH]
         up = gu[o, :, FH:2 * FH]
         sig = 1.0 / (1.0 + jnp.exp(-gate))
@@ -242,22 +251,37 @@
         send(dd.at[2, o, :, HALF:W], hb.at[o], cxs.at[o, 1], cxr.at[o, 1], dev(dx=NX - 1))
         for r in (1, 3, 0):
             dd[r, o] = dot_nt(both, wgu[r]).astype(BF)
+            if r == 1:
+                at = slice(HALF, W)
+                send(dd.at[1, o, :, at], fl.at[o, :, at], cxs.at[o, 4], cxr.at[o, 4], dev(dx=1))
+            if r == 3:
+                at = slice(0, HALF)
+                send(
+                    dd.at[3, o, :, at], fr.at[o, :, at], cxs.at[o, 5], cxr.at[o, 5], dev(dx=NX - 1)
+                )
 
     def sum_second(o):
         arrived(ha.at[o], cxr.at[o, 0])
         dd[1, o, :, 0:HALF] = (dd[1, o, :, 0:HALF].astype(F32) + ha[o].astype(F32)).astype(BF)
-        send(dd.at[1, o], fl.at[o], cxs.at[o, 2], cxr.at[o, 2], dev(dx=1))
+        send(
+            dd.at[1, o, :, 0:HALF], fl.at[o, :, 0:HALF], cxs.at[o, 2], cxr.at[o, 2], dev(dx=1)
+        )
         arrived(hb.at[o], cxr.at[o, 1])
         dd[3, o, :, HALF:W] = (dd[3, o, :, HALF:W].astype(F32) + hb[o].astype(F32)).astype(BF)
-        send(dd.at[3, o], fr.at[o], cxs.at[o, 3], cxr.at[o, 3], dev(dx=NX - 1))
+        send(
+            dd.at[3, o, :, HALF:W], fr.at[o, :, HALF:W],
+            cxs.at[o, 3], cxr.at[o, 3], dev(dx=NX - 1),
+        )
 
     def sum_third(o):
         g = (NY - o) % NY
         for k, d in enumerate((1, 3, 2)):
             arrived(gx.at[NX - d, o], gxr.at[o, k])
         parts = (gx[0, o] + gx[1, o]) + (gx[2, o] + gx[3, o])
-        arrived(fl.at[o], cxr.at[o, 2])
-        arrived(fr.at[o], cxr.at[o, 3])
+        arrived(fl.at[o, :, HALF:W], cxr.at[o, 4])
+        arrived(fr.at[o, :, 0:HALF], cxr.at[o, 5])
+        arrived(fl.at[o, :, 0:HALF], cxr.at[o, 2])
+        arrived(fr.at[o, :, HALF:W], cxr.at[o, 3])
         total = dd[0, o].astype(F32) + fl[o].astype(F32) + fr[o].astype(F32)
         if o == 0:
             qq[0] = total.astype(BF)
@@ -270,12 +294,15 @@
 
     for j in range(NY):
         backward(BACK[j])
+        if j < NY - 2:
+            arrived(rg.at[BACK[j + 1]], yrg.at[BACK[j + 1]])
+            x_grad(BACK[j + 1])
+            sum_second(BACK[j])
+        if j == NY - 1:
+            sum_second(BACK[2])
+            sum_second(BACK[3])
         if j:
-            sum_second(BACK[j - 1])
-        if j > 1:
-            sum_third(BACK[j - 2])
-    sum_second(BACK[3])
-    sum_third(BACK[2])
+            sum_third(BACK[j - 1])
 
     for g in range(NY):
         e = (z * NY + (y + g) % NY) * NC + c
@@ -405,11 +432,11 @@
     D = pltpu.SemaphoreType.DMA
     n_tok = SLOTS * ROWS
     scratch = [
-        V((SLOTS, ROWS, W + META), BF), V((SLOTS, ROWS, W), BF),
+        V((SLOTS, ROWS, W + META), BF), V((SLOTS, ROWS, 2 * W), BF),
         V((NY * CH, n_tok), BF), V((NY, n_tok, CH), BF),
-        V((NY - 1, CH, W + META), BF), V((NY - 1, CH, W), BF),
-        V((NY, CH, W + META), BF), V((NY, CH, W), BF),
-        V((NX - 1, NY, CH, W), BF), V((NX - 1, NY, CH, W), BF),
+        V((NY - 1, CH, W + META), BF), V((NY - 1, CH, 2 * W), BF),
+        V((NY, CH, W + META), BF), V((NY, CH, 2 * W), BF),
+        V((NX - 1, NY, CH, W), BF), V((2, NY, CH, W), BF),
         V((NX, W, 2 * FH), BF), V((NX, FH, W), BF),
         V((NY, CH, 2 * FH), F32), V((NX, NY, CH, W), BF),
         V((NY, CH, HALF), BF), V((NY, CH, HALF), BF), V((NY, CH, W), BF), V((NY, CH, W), BF),
@@ -421,10 +448,11 @@
         D((12,)),
         D((16,)), D((16,)), D((17,)), D((17,)),
         D((4,)), D((4,)), D((4,)), D((4,)),
-        D((4, 4)), D((4, 4)), D((4, 4)), D((4, 4)),
-        D((4, 4)), D((4, 4)), D((4, 3)), D((4, 3)),
+        D((4, 6)), D((4, 2)), D((4, 6)), D((4, 2)),
+        D((4, 6)), D((4, 6)), D((4, 3)), D((4, 3)),
         D((4,)), D((4,)), D((4,)), D((4,)),
         D((8,)), D((8,)), D((2, 2, 4)), D((2, 2, 4)), D((16,)), D((16,)),
+        D((1,)), D((1,)),
     ]
     return pl.pallas_call(
         kernel,

time: 189 us -> 188 us (level)
  no operation moved by 1% of the time
where the time goes in v4:
time: 188 us
  Pallas kernels  181 us (96%)
  local copies, waits for them, and re-layouts  5.69 us (3%)
    pallas_call x1, Pallas kernels, body(): pl.pallas_call(kernel, out_shape=(jax.ShapeDtypeStruct(tokens.shape, BF),...  181 us

profile of v4, /device:TPU:1, one launch (start us, length us, event | category | flops | bytes accessed | tf_op | source)
XLA Modules:
  0.0 187.5 jit_solution(11392587808085995720)
XLA Ops:
  0.6 1.4 copy.12.ids_ref
  2.0 1.4 copy.13.rw_ref
  3.4 181.2 %shard_map.86 = (bf16[64,1024]{1,0:T(8,128)(2,1)}, bf16[64,8]{1,0:T(8,128)(2,1)}) custom-call(bf16[64,1024]{1,0:T(8,128)(2,1)} %tok_ref.1, bf16[64,1024]{1,0:T(8,128)(2,1)} %grd_ref.1, s32[64,8]{1,0:T(8,128)} %copy.12.ids_ref, f32[64,8]{1,0:T(8,128)} %copy.13.rw_ref, bf16[1,4096,384]{2,1,0:T(8,128)(2,1)} %wg_ref.1, bf16[1,4096,384]{2,1,0:T(8,128)(2,1)} %wu_ref.1, ...), custom_call_target="tpu_custom_call" | custom-call | tf_op jit(solution)/shard_map/pallas_call | solution.py:457
  184.6 1.4 copy.14
  186.0 1.6 copy.16
